TPU v7x, 128 devices: a whole 4x4x4 slice. The times are simulated.
128 devices in a mesh: ctx: 32 (over y, z_lo, x), head: 4 (over z_hi, core).
Axes of the slice: x: 4, y: 4, z: 4 (z_hi: 2, z_lo: 2; z = z_hi * 2 + z_lo), core: 2. Of those that a mesh axis runs over, the one named last changes fastest.
Arguments:
- kda_inputs: bfloat16 [3, 4096, 4096], P(None, 'ctx', 'head'), may hold values from -4 to 4
- gate_log: float32 [4096, 4096], P('ctx', 'head'), may hold values from -2.2 to 0
- beta: float32 [4096, 32], P('ctx', 'head'), may hold values from 0.1 to 0.9
- conv_weight: float32 [3, 4, 4096], P(None, None, 'head'), may hold values from -3 to 3
- kda_out_weight: bfloat16 [4096, 2304], P('head'), may hold values from -3 to 3
- residual: bfloat16 [4096, 2304], P('ctx'), may hold values from -3 to 3
- norm_gain: float32 [2304], replicated, may hold values from 0.1 to 1.9
- latent_weight: bfloat16 [2304, 512], replicated, may hold values from -0.125 to 0.125
- latent_gain: float32 [512], replicated, may hold values from 0.1 to 1.9
- query_weight: bfloat16 [2304, 2048], P(None, 'head'), may hold values from -0.27083333 to 0.27083333
- up_weight: bfloat16 [512, 2, 2048], P(None, None, 'head'), may hold values from -0.5745243 to 0.5745243
Outputs:
- stream_out: bfloat16 [4096, 2304], P('ctx')
- attention_out: bfloat16 [4096, 2048], P('ctx', 'head')
All inputs are finite; a program needn't handle non-finite values.
Results may differ from a plain program's by a relative error of at most 0.04.
Values may be sent and summed in bfloat16 or wider, within the bound.
A program may use at most 128 MiB of HBM per device.

v0:
```python
import math

import jax
import jax.numpy as jnp
from jax import lax
from jax.sharding import PartitionSpec as P

DK = 128
CONV = 4
DH = 128


eps_norm = 1e-06
highest_precision = lax.Precision.HIGHEST


def passed_along(block, axis, distance):
    devices = range(lax.axis_size(axis))
    route = [(i - distance, i) for i in devices if i - distance in devices]
    return lax.ppermute(block, axis, route)


def rounded(values):
    return lax.optimization_barrier(values.astype(jnp.bfloat16))


def unit_heads(activated):
    grouped = activated.reshape(activated.shape[0], -1, DK)
    scaled = grouped * lax.rsqrt(jnp.sum(grouped * grouped, axis=-1, keepdims=True) + eps_norm)
    return scaled.reshape(activated.shape)


def prepare(stream, norm_gain, latent_weight, latent_gain):
    widened = stream.astype(jnp.float32)
    normed = (
        widened
        * lax.rsqrt(jnp.mean(widened * widened, axis=-1, keepdims=True) + eps_norm)
        * norm_gain
    ).astype(jnp.bfloat16)
    latent_pre = jnp.dot(normed, latent_weight, preferred_element_type=jnp.float32)
    latent = (
        latent_pre
        * lax.rsqrt(jnp.mean(latent_pre * latent_pre, axis=-1, keepdims=True) + eps_norm)
        * latent_gain
    ).astype(jnp.bfloat16)
    return (normed, latent)


def span_layout(values, span_rows):
    length, channel_count = values.shape
    return values.reshape(length // span_rows, span_rows, channel_count // DK, DK).transpose(
        0, 2, 1, 3
    )


def matmul_heads(left, right):
    return jnp.einsum("hij,hjk->hik", left, right, precision=highest_precision)


def delta_rule(kda_query, kda_key, kda_value, gate_log, beta):
    span_rows = 32
    length, channel_count = gate_log.shape
    heads = channel_count // DK
    queries = span_layout(kda_query.astype(jnp.float32), span_rows)
    keys_unit = span_layout(kda_key.astype(jnp.float32), span_rows)
    values_new = span_layout(kda_value.astype(jnp.float32), span_rows)
    cumulative = jnp.cumsum(span_layout(gate_log, span_rows), axis=2)
    rates = beta.reshape(length // span_rows, span_rows, heads).transpose(0, 2, 1)[..., None]
    growth = jnp.exp(cumulative)
    final_log = cumulative[:, :, -1:, :]
    keys_grown = keys_unit * growth
    keys_shrunk = keys_unit * jnp.exp(-cumulative)
    queries_grown = queries * growth
    keys_final = keys_unit * jnp.exp(final_log - cumulative)
    strict = jnp.tril(jnp.ones((span_rows, span_rows), jnp.float32), -1)
    inclusive = jnp.tril(jnp.ones((span_rows, span_rows), jnp.float32))
    coupling = (
        jnp.einsum("nhtc,nhsc->nhts", keys_grown, keys_shrunk, precision=highest_precision)
        * jnp.swapaxes(rates, -1, -2)
        * strict
    )
    system = coupling + jnp.eye(span_rows, dtype=jnp.float32)
    solved = jax.scipy.linalg.solve_triangular(
        system, jnp.concatenate([values_new, keys_grown], axis=-1), lower=True, unit_diagonal=True
    )
    fresh = solved[..., :DK] * rates
    carried = solved[..., DK:] * rates
    eye_key = jnp.eye(DK, dtype=jnp.float32)
    transition = jnp.exp(final_log[:, :, 0, :])[..., :, None] * eye_key - jnp.einsum(
        "nhsk,nhsv->nhkv", keys_final, carried, precision=highest_precision
    )
    offset = jnp.einsum("nhsk,nhsv->nhkv", keys_final, fresh, precision=highest_precision)
    mixing = (
        jnp.einsum("nhtc,nhsc->nhts", queries_grown, keys_shrunk, precision=highest_precision)
        * inclusive
    )

    def compose(accumulated, span_parts):
        span_move, span_shift = span_parts
        return (
            (
                matmul_heads(span_move, accumulated[0]),
                matmul_heads(span_move, accumulated[1]) + span_shift,
            ),
            None,
        )

    identity_map = jnp.broadcast_to(eye_key, (heads, DK, DK))
    zero_map = jnp.zeros((heads, DK, DK), jnp.float32)
    (device_move, device_shift), _ = lax.scan(
        compose, (identity_map, zero_map), (transition, offset)
    )
    return (device_move, device_shift, (transition, offset, fresh, carried, queries_grown, mixing))


def emit_spans(start_state, span_data):

    def emit(recurrent_state, span_parts):
        span_move, span_shift, fresh_state_term, carried_state_term, query_term, mixing_part = (
            span_parts
        )
        state_update = fresh_state_term - jnp.einsum(
            "orm,omj->orj", carried_state_term, recurrent_state, precision=highest_precision
        )
        produced_output = jnp.einsum(
            "fmb,fbi->fmi", query_term, recurrent_state, precision=highest_precision
        ) + jnp.einsum("hts,hsv->htv", mixing_part, state_update, precision=highest_precision)
        return (matmul_heads(span_move, recurrent_state) + span_shift, produced_output)

    _, outputs = lax.scan(emit, start_state, span_data)
    block_count, heads, span_rows, _ = outputs.shape
    return (
        outputs.transpose(0, 2, 1, 3)
        .reshape(block_count * span_rows, heads * DK)
        .astype(jnp.bfloat16)
    )


def per_device(
    kda_inputs,
    gate_log,
    beta,
    conv_weight,
    kda_out_weight,
    residual,
    norm_gain,
    latent_weight,
    latent_gain,
    query_weight,
    up_weight,
):
    length = residual.shape[0]
    edge_rows = kda_inputs[:, length - (CONV - 1) :, :]
    earlier_rows = passed_along(edge_rows, "ctx", 1)
    extended = jnp.concatenate([earlier_rows, kda_inputs], axis=1).astype(jnp.float32)
    running = jnp.zeros(kda_inputs.shape, jnp.float32)
    for tap_index in range(CONV):
        running = (
            running
            + conv_weight[:, tap_index, None, :] * extended[:, tap_index : tap_index + length, :]
        )
    activated = jax.nn.silu(running)
    kda_query = rounded(unit_heads(activated[0]) * DK ** (-0.5))
    kda_key = rounded(unit_heads(activated[1]))
    kda_value = rounded(activated[2])
    device_move, device_shift, span_data = delta_rule(kda_query, kda_key, kda_value, gate_log, beta)
    heads = device_move.shape[0]

    def relay(step_index, incoming):
        leaving = matmul_heads(device_move, incoming) + device_shift
        return passed_along(leaving, "ctx", 1)

    start_state = lax.fori_loop(
        0, lax.axis_size("ctx") - 1, relay, jnp.zeros((heads, DK, DK), jnp.float32)
    )
    kda_core = emit_spans(start_state, span_data)
    partial_proj = jnp.dot(kda_core, kda_out_weight, preferred_element_type=jnp.float32)
    summed = lax.psum(partial_proj, "head")
    stream_out = (residual.astype(jnp.float32) + summed).astype(jnp.bfloat16)
    normed, latent = prepare(stream_out, norm_gain, latent_weight, latent_gain)
    mla_query = jnp.dot(normed, query_weight, preferred_element_type=jnp.float32).astype(
        jnp.bfloat16
    )
    query_heads = mla_query.reshape(length, -1, DH)
    heads_mla = query_heads.shape[1]
    flat_up = up_weight.reshape(up_weight.shape[0], -1)
    my_first = lax.axis_index("ctx") * length
    query_positions = my_first + jnp.arange(length, dtype=jnp.int32)
    initial = (
        jnp.full((heads_mla, length), -1e30, jnp.float32),
        jnp.zeros((heads_mla, length), jnp.float32),
        jnp.zeros((heads_mla, length, DH), jnp.float32),
    )
    piece = lax.all_gather(latent, "ctx", axis=0, tiled=True)
    piece_rows = piece.shape[0]
    block_rows = math.gcd(piece_rows, 512)
    blocks = piece.reshape(piece_rows // block_rows, block_rows, piece.shape[1])

    def one_block(state_parts, block_parts):
        block_index, latent_block = block_parts
        running_peak, running_total, running_mixed = state_parts
        paired = (
            jnp.dot(latent_block, flat_up, preferred_element_type=jnp.float32)
            .astype(jnp.bfloat16)
            .reshape(block_rows, 2, heads_mla, DH)
        )
        scores = jnp.einsum(
            "qhd,khd->hqk", query_heads, paired[:, 0], preferred_element_type=jnp.float32
        ) * DH ** (-0.5)
        key_positions = block_index * block_rows + jnp.arange(block_rows, dtype=jnp.int32)
        allowed = key_positions[None, :] <= query_positions[:, None]
        new_peak = jnp.maximum(running_peak, jnp.max(jnp.where(allowed, scores, -1e30), axis=-1))
        weights = jnp.where(allowed, jnp.exp(scores - new_peak[..., None]), 0.0)
        factor = jnp.exp(running_peak - new_peak)
        new_total = running_total * factor + jnp.sum(weights, axis=-1)
        new_mixed = running_mixed * factor[..., None] + jnp.einsum(
            "hqk,khd->hqd",
            weights.astype(jnp.bfloat16),
            paired[:, 1],
            preferred_element_type=jnp.float32,
        )
        return ((new_peak, new_total, new_mixed), None)

    def attend(state_parts):
        return lax.scan(
            one_block, state_parts, (jnp.arange(piece_rows // block_rows, dtype=jnp.int32), blocks)
        )[0]

    final_peak, final_total, final_mixed = lax.cond(
        jnp.int32(0) < my_first + length, attend, lambda state_parts: state_parts, initial
    )
    attention_out = (
        (final_mixed / final_total[..., None])
        .transpose(1, 0, 2)
        .reshape(length, heads_mla * DH)
        .astype(jnp.bfloat16)
    )
    return (stream_out, attention_out)


def solution(mesh):
    in_specs = (
        P(None, "ctx", "head"),
        P("ctx", "head"),
        P("ctx", "head"),
        P(None, None, "head"),
        P("head", None),
        P("ctx", None),
        P(),
        P(),
        P(),
        P(None, "head"),
        P(None, None, "head"),
    )
    out_specs = (P("ctx", None), P("ctx", "head"))
    return jax.shard_map(
        per_device, mesh=mesh, in_specs=in_specs, out_specs=out_specs, check_vma=False
    )
```

profile of v0, /device:TPU:0, one launch (start us, length us, event | category | flops | bytes accessed | tf_op | source)
XLA Modules:
  0.0 1073.1 jit_solution(16578880759625997897)
XLA Ops:
  16.0 7.6 fusion.56
  46.1 80.2 %custom-call.4 = f32[4,8,1,32,32]{3,4,2,1,0:T(8,128)} custom-call(f32[4,8,1,32,32]{4,3,2,1,0:T(8,128)} %fusion.45), custom_call_target="InvertDiagBlocksLowerTriangular" | custom-call | tf_op jit(solution)/shard_map/jit(_solve_triangular)/vmap(vmap())/triangular_solve | solution.py:83
  139.7 14.7 %while.52 = (s32[]{:T(128)}, f32[8,128,128]{2,1,0:T(8,128)S(1)}, f32[8,128,128]{2,1,0:T(8,128)S(1)}, f32[4,8,128,128]{3,2,1,0:T(8,128)}, f32[4,8,128,128]{3,2,1,0:T(8,128)}, /*index=5*/s32[]{:T(128)}, s32[]{:T(128)}) while((s32[]{:T(128)}, f32[8,128,128]{2,1,0:T(8,128)S(1)}, f32[8,128,128]{2,1,0:T(8,128)S(1)}, ...), condition=%wide.region_3.4_spmd.clone, body=%wide.region_2.3_spmd.clone.sunk | while | flops 402915328 | bytes 5768791 | solution.py:110
  157.9 539.7 %while.50 = (s32[]{:T(128)}, f32[8,128,128]{2,1,0:T(8,128)S(1)}, f32[8,128,128]{2,1,0:T(8,128)S(1)}, f32[8,128,128]{2,1,0:T(8,128)}, s32[]{:T(128)}) while((s32[]{:T(128)}, f32[8,128,128]{2,1,0:T(8,128)S(1)}, f32[8,128,128]{2,1,0:T(8,128)S(1)}, f32[8,128,128]{2,1,0:T(8,128)}, s32[]{:T(128)}) %tuple.119), condition=%wide.region_5.6_spmd, body=%wide.region_4.5_spmd.sunk | while | flops 201457664 | bytes 4194405 | solution.py:173
  163.5 11.2 %collective-permute-done = f32[8,128,128]{2,1,0:T(8,128)S(1)} collective-permute-done((f32[8,128,128]{2,1,0:T(8,128)}, f32[8,128,128]{2,1,0:T(8,128)S(1)}, u32[]{:S(2)}, u32[]{:S(2)}) %collective-permute-start) | collective-permute-done | bytes 524320 | tf_op jit(solution)/shard_map/while/body/eval_jaxpr/ppermute | solution.py:20
  181.5 10.3 collective-permute-done
  198.6 9.3 collective-permute-done
  214.7 8.4 collective-permute-done
  230.0 7.5 collective-permute-done
  245.9 7.0 collective-permute-done
  255.4 6.4 collective-permute-start
  261.8 7.0 collective-permute-done
  271.3 6.4 collective-permute-start
  277.7 7.0 collective-permute-done
  287.2 6.4 collective-permute-start
  293.6 7.0 collective-permute-done
  303.0 6.4 collective-permute-start
  309.5 7.5 collective-permute-done
  319.5 6.7 collective-permute-start
  326.2 8.5 collective-permute-done
  337.2 7.2 collective-permute-start
  344.4 9.6 collective-permute-done
  356.5 7.3 collective-permute-start
  363.9 10.7 collective-permute-done
  377.0 7.3 collective-permute-start
  384.3 11.9 %collective-permute-done = f32[8,128,128]{2,1,0:T(8,128)S(1)} collective-permute-done((f32[8,128,128]{2,1,0:T(8,128)}, f32[8,128,128]{2,1,0:T(8,128)S(1)}, u32[]{:S(2)}, u32[]{:S(2)}) %collective-permute-start) | collective-permute-done | bytes 524320 | tf_op jit(solution)/shard_map/while/body/eval_jaxpr/ppermute | solution.py:20
  398.7 7.4 collective-permute-start
  406.1 12.1 %collective-permute-done = f32[8,128,128]{2,1,0:T(8,128)S(1)} collective-permute-done((f32[8,128,128]{2,1,0:T(8,128)}, f32[8,128,128]{2,1,0:T(8,128)S(1)}, u32[]{:S(2)}, u32[]{:S(2)}) %collective-permute-start) | collective-permute-done | bytes 524320 | tf_op jit(solution)/shard_map/while/body/eval_jaxpr/ppermute | solution.py:20
  420.7 6.8 collective-permute-start
  427.5 11.0 %collective-permute-done = f32[8,128,128]{2,1,0:T(8,128)S(1)} collective-permute-done((f32[8,128,128]{2,1,0:T(8,128)}, f32[8,128,128]{2,1,0:T(8,128)S(1)}, u32[]{:S(2)}, u32[]{:S(2)}) %collective-permute-start) | collective-permute-done | bytes 524320 | tf_op jit(solution)/shard_map/while/body/eval_jaxpr/ppermute | solution.py:20
  446.7 9.7 collective-permute-done
  458.9 6.4 collective-permute-start
  465.3 8.8 collective-permute-done
  476.6 6.4 collective-permute-start
  483.1 7.9 collective-permute-done
  493.5 6.4 collective-permute-start
  499.9 7.0 collective-permute-done
  509.4 6.4 collective-permute-start
  515.8 7.0 collective-permute-done
  525.3 6.4 collective-permute-start
  531.7 7.0 collective-permute-done
  541.2 7.1 collective-permute-start
  548.2 7.0 collective-permute-done
  557.7 7.3 collective-permute-start
  565.0 7.0 collective-permute-done
  574.5 7.3 collective-permute-start
  581.8 7.0 collective-permute-done
  591.3 7.3 collective-permute-start
  598.6 7.0 collective-permute-done
  608.1 7.3 collective-permute-start
  615.4 7.5 collective-permute-done
  625.4 7.5 collective-permute-start
  633.0 8.5 collective-permute-done
  644.1 8.2 collective-permute-start
  652.3 9.6 collective-permute-done
  664.4 8.5 collective-permute-start
  672.9 7.0 collective-permute-done
  682.4 8.3 collective-permute-start
  690.6 7.0 collective-permute-done
  697.6 25.0 %while.51 = (s32[]{:T(128)}, f32[8,128,128]{2,1,0:T(8,128)S(1)}, bf16[4,8,32,128]{3,2,1,0:T(8,128)(2,1)}, f32[4,8,128,128]{3,2,1,0:T(8,128)}, f32[4,8,128,128]{3...) while((s32[]{:T(128)}, f32[8,128,128]{2,1,0:T(8,128)S(1)}, ...), condition=%wide.region_8.9_spmd, body=%wide.region_7.8_spmd.sunk | while | flops 314769408 | bytes 7474845 | solution.py:130
  727.9 82.7 %all-reduce.2.cloned.1.call-done = f32[128,2304]{1,0:T(8,128)} async-done(((f32[128,2304]{1,0:T(8,128)}), f32[128,2304]{1,0:T(8,128)}) %all-reduce.2.cloned.1.call-update) | async-done | bytes 1179664 | tf_op jit(solution)/shard_map/psum | solution.py:178
  816.3 154.4 %all-gather.2.cloned.1.call-done = bf16[4096,512]{1,0:T(8,128)(2,1)} async-done(((bf16[128,512]{1,0:T(8,128)(2,1)}), bf16[4096,512]{1,0:T(8,128)(2,1)}) %all-gather.2.cloned.1.call-update) | async-done | bytes 4194320 | tf_op jit(solution)/shard_map/all_gather | solution.py:194
  970.7 93.8 %conditional.1 = (f32[4,128]{1,0:T(4,128)}, f32[4,128,128]{2,1,0:T(8,128)}) conditional(s32[]{:T(128)} %convert_element_type.88, () %tuple.35, (bf16[4096,512]{1,0:T(8,128)(2,1)}, bf16[512,2,512]{2,1,0:T(2,128)(2,1)S(1)}, bf16[128,512]{1,0:T(8,128)(2,1)S(1)}, s32[]{:T(128)}, s32[128]{0:T(128)S(1)}) %tuple.124), branch_computations={%region_12.13_spmd, %region_13.18_spmd} | conditional | flops 674237568 | bytes 15112533 | solution.py:229
  972.9 91.6 %while.49 = (s32[]{:T(128)}, f32[4,128]{1,0:T(4,128)S(1)}, f32[4,128]{1,0:T(4,128)}, f32[4,128,128]{2,1,0:T(8,128)}, s32[8]{0:T(128)S(1)}, /*index=5*/s32[128]{0...) while((s32[]{:T(128)}, f32[4,128]{1,0:T(4,128)S(1)}, ...), condition=%wide.region_17.17_spmd.clone, body=%wide.region_14.16_spmd.clone.sunk | while | flops 674237440 | bytes 12489913 | solution.py:225
  (320 shorter events, 297.7 us)
Async XLA Ops:
  7.2 805.0 %copy-start = (bf16[2304,512]{1,0:T(8,128)(2,1)S(1)}, bf16[2304,512]{1,0:T(8,128)(2,1)}, u32[]{:S(2)}) copy-start(bf16[2304,512]{1,0:T(8,128)(2,1)} %param.28) | copy-start | bytes 7077892
  7.2 17.2 %copy-start.23 = (f32[3,4,1024]{2,1,0:T(4,128)S(1)}, f32[3,4,1024]{2,1,0:T(4,128)}, u32[]{:S(2)}) copy-start(f32[3,4,1024]{2,1,0:T(4,128)} %param.24) | copy-start | bytes 147460
  7.2 803.4 %all-reduce.2.cloned.1.call-start = ((), (), s32[]{:S(2)}) async-start(), calls=%async_computation | async-start | bytes 2359296 | tf_op jit(solution)/shard_map/psum | solution.py:178
  8.8 18.9 %collective-permute-start.1 = (bf16[3,3,1024]{2,1,0:T(4,128)(2,1)}, bf16[3,3,1024]{2,1,0:T(4,128)(2,1)}, u32[]{:S(2)}, u32[]{:S(2)}) collective-permute-start(bf16[3,3,1024]{2,1,0:T(4,128)(2,1)} %slice.60), channel_id=1, source_target_pairs={{0,4},{4,8},{8,12},{12,16},{16,20},{20,24},{24,28},{28,32},{32,36}... | collective-permute-start | bytes 55304 | tf_op jit(solution)/shard_map/ppermute | solution.py:20
  23.6 110.9 %copy-start.2 = (f32[4,8,32,128]{3,1,2,0:T(8,128)}, f32[4,8,32,128]{3,1,2,0:T(8,128)S(1)}, u32[]{:S(2)}) copy-start(f32[4,8,32,128]{3,1,2,0:T(8,128)S(1)} %fusion.56) | copy-start | bytes 1572868
  30.0 2.6 copy-start.5
  42.1 1.3 copy-start.3
  42.2 1.9 copy-start.16
  42.2 1.9 copy-start.20
  42.2 1.9 copy-start.21
  42.3 1.9 copy-start.22
  42.3 1.9 copy-start.24
  126.3 1.3 copy-start.9
  126.3 1.3 copy-start.13
  128.9 5.6 copy-start.6
  128.9 5.6 copy-start.7
  129.7 4.8 copy-start.19
  139.7 14.7 %copy-start.18 = (f32[32,32]{1,0:T(8,128)S(1)}, f32[32,32]{1,0:T(8,128)}, u32[]{:S(2)}) copy-start(f32[32,32]{1,0:T(8,128)} %fusion.70) | copy-start | bytes 12292
  154.5 3.4 copy-start.1
  160.7 14.0 %collective-permute-start = (f32[8,128,128]{2,1,0:T(8,128)}, f32[8,128,128]{2,1,0:T(8,128)S(1)}, u32[]{:S(2)}, u32[]{:S(2)}) collective-permute-start(f32[8,128,128]{2,1,0:T(8,128)} %convolution_add_fusion.9), channel_id=1, source_target_pairs={{0,4},{4,8},{8,12},{12,16},{16,20},{20,24},{24,28},{28,32},{32,36}... | collective-permute-start | bytes 1572872 | tf_op jit(solution)/shard_map/while/body/eval_jaxpr/ppermute | solution.py:20
  177.2 14.6 %collective-permute-start = (f32[8,128,128]{2,1,0:T(8,128)}, f32[8,128,128]{2,1,0:T(8,128)S(1)}, u32[]{:S(2)}, u32[]{:S(2)}) collective-permute-start(f32[8,128,128]{2,1,0:T(8,128)} %convolution_add_fusion.9), channel_id=1, source_target_pairs={{0,4},{4,8},{8,12},{12,16},{16,20},{20,24},{24,28},{28,32},{32,36}... | collective-permute-start | bytes 1572872 | tf_op jit(solution)/shard_map/while/body/eval_jaxpr/ppermute | solution.py:20
  194.3 13.6 %collective-permute-start = (f32[8,128,128]{2,1,0:T(8,128)}, f32[8,128,128]{2,1,0:T(8,128)S(1)}, u32[]{:S(2)}, u32[]{:S(2)}) collective-permute-start(f32[8,128,128]{2,1,0:T(8,128)} %convolution_add_fusion.9), channel_id=1, source_target_pairs={{0,4},{4,8},{8,12},{12,16},{16,20},{20,24},{24,28},{28,32},{32,36}... | collective-permute-start | bytes 1572872 | tf_op jit(solution)/shard_map/while/body/eval_jaxpr/ppermute | solution.py:20
  210.4 12.7 %collective-permute-start = (f32[8,128,128]{2,1,0:T(8,128)}, f32[8,128,128]{2,1,0:T(8,128)S(1)}, u32[]{:S(2)}, u32[]{:S(2)}) collective-permute-start(f32[8,128,128]{2,1,0:T(8,128)} %convolution_add_fusion.9), channel_id=1, source_target_pairs={{0,4},{4,8},{8,12},{12,16},{16,20},{20,24},{24,28},{28,32},{32,36}... | collective-permute-start | bytes 1572872 | tf_op jit(solution)/shard_map/while/body/eval_jaxpr/ppermute | solution.py:20
  225.7 11.8 %collective-permute-start = (f32[8,128,128]{2,1,0:T(8,128)}, f32[8,128,128]{2,1,0:T(8,128)S(1)}, u32[]{:S(2)}, u32[]{:S(2)}) collective-permute-start(f32[8,128,128]{2,1,0:T(8,128)} %convolution_add_fusion.9), channel_id=1, source_target_pairs={{0,4},{4,8},{8,12},{12,16},{16,20},{20,24},{24,28},{28,32},{32,36}... | collective-permute-start | bytes 1572872 | tf_op jit(solution)/shard_map/while/body/eval_jaxpr/ppermute | solution.py:20
  240.0 12.9 %collective-permute-start = (f32[8,128,128]{2,1,0:T(8,128)}, f32[8,128,128]{2,1,0:T(8,128)S(1)}, u32[]{:S(2)}, u32[]{:S(2)}) collective-permute-start(f32[8,128,128]{2,1,0:T(8,128)} %convolution_add_fusion.9), channel_id=1, source_target_pairs={{0,4},{4,8},{8,12},{12,16},{16,20},{20,24},{24,28},{28,32},{32,36}... | collective-permute-start | bytes 1572872 | tf_op jit(solution)/shard_map/while/body/eval_jaxpr/ppermute | solution.py:20
  255.4 13.4 %collective-permute-start = (f32[8,128,128]{2,1,0:T(8,128)}, f32[8,128,128]{2,1,0:T(8,128)S(1)}, u32[]{:S(2)}, u32[]{:S(2)}) collective-permute-start(f32[8,128,128]{2,1,0:T(8,128)} %convolution_add_fusion.9), channel_id=1, source_target_pairs={{0,4},{4,8},{8,12},{12,16},{16,20},{20,24},{24,28},{28,32},{32,36}... | collective-permute-start | bytes 1572872 | tf_op jit(solution)/shard_map/while/body/eval_jaxpr/ppermute | solution.py:20
  271.3 13.4 %collective-permute-start = (f32[8,128,128]{2,1,0:T(8,128)}, f32[8,128,128]{2,1,0:T(8,128)S(1)}, u32[]{:S(2)}, u32[]{:S(2)}) collective-permute-start(f32[8,128,128]{2,1,0:T(8,128)} %convolution_add_fusion.9), channel_id=1, source_target_pairs={{0,4},{4,8},{8,12},{12,16},{16,20},{20,24},{24,28},{28,32},{32,36}... | collective-permute-start | bytes 1572872 | tf_op jit(solution)/shard_map/while/body/eval_jaxpr/ppermute | solution.py:20
  287.2 13.4 %collective-permute-start = (f32[8,128,128]{2,1,0:T(8,128)}, f32[8,128,128]{2,1,0:T(8,128)S(1)}, u32[]{:S(2)}, u32[]{:S(2)}) collective-permute-start(f32[8,128,128]{2,1,0:T(8,128)} %convolution_add_fusion.9), channel_id=1, source_target_pairs={{0,4},{4,8},{8,12},{12,16},{16,20},{20,24},{24,28},{28,32},{32,36}... | collective-permute-start | bytes 1572872 | tf_op jit(solution)/shard_map/while/body/eval_jaxpr/ppermute | solution.py:20
  303.0 13.9 %collective-permute-start = (f32[8,128,128]{2,1,0:T(8,128)}, f32[8,128,128]{2,1,0:T(8,128)S(1)}, u32[]{:S(2)}, u32[]{:S(2)}) collective-permute-start(f32[8,128,128]{2,1,0:T(8,128)} %convolution_add_fusion.9), channel_id=1, source_target_pairs={{0,4},{4,8},{8,12},{12,16},{16,20},{20,24},{24,28},{28,32},{32,36}... | collective-permute-start | bytes 1572872 | tf_op jit(solution)/shard_map/while/body/eval_jaxpr/ppermute | solution.py:20
  319.5 15.2 %collective-permute-start = (f32[8,128,128]{2,1,0:T(8,128)}, f32[8,128,128]{2,1,0:T(8,128)S(1)}, u32[]{:S(2)}, u32[]{:S(2)}) collective-permute-start(f32[8,128,128]{2,1,0:T(8,128)} %convolution_add_fusion.9), channel_id=1, source_target_pairs={{0,4},{4,8},{8,12},{12,16},{16,20},{20,24},{24,28},{28,32},{32,36}... | collective-permute-start | bytes 1572872 | tf_op jit(solution)/shard_map/while/body/eval_jaxpr/ppermute | solution.py:20
  337.2 16.8 %collective-permute-start = (f32[8,128,128]{2,1,0:T(8,128)}, f32[8,128,128]{2,1,0:T(8,128)S(1)}, u32[]{:S(2)}, u32[]{:S(2)}) collective-permute-start(f32[8,128,128]{2,1,0:T(8,128)} %convolution_add_fusion.9), channel_id=1, source_target_pairs={{0,4},{4,8},{8,12},{12,16},{16,20},{20,24},{24,28},{28,32},{32,36}... | collective-permute-start | bytes 1572872 | tf_op jit(solution)/shard_map/while/body/eval_jaxpr/ppermute | solution.py:20
  356.5 18.0 %collective-permute-start = (f32[8,128,128]{2,1,0:T(8,128)}, f32[8,128,128]{2,1,0:T(8,128)S(1)}, u32[]{:S(2)}, u32[]{:S(2)}) collective-permute-start(f32[8,128,128]{2,1,0:T(8,128)} %convolution_add_fusion.9), channel_id=1, source_target_pairs={{0,4},{4,8},{8,12},{12,16},{16,20},{20,24},{24,28},{28,32},{32,36}... | collective-permute-start | bytes 1572872 | tf_op jit(solution)/shard_map/while/body/eval_jaxpr/ppermute | solution.py:20
  377.0 19.2 %collective-permute-start = (f32[8,128,128]{2,1,0:T(8,128)}, f32[8,128,128]{2,1,0:T(8,128)S(1)}, u32[]{:S(2)}, u32[]{:S(2)}) collective-permute-start(f32[8,128,128]{2,1,0:T(8,128)} %convolution_add_fusion.9), channel_id=1, source_target_pairs={{0,4},{4,8},{8,12},{12,16},{16,20},{20,24},{24,28},{28,32},{32,36}... | collective-permute-start | bytes 1572872 | tf_op jit(solution)/shard_map/while/body/eval_jaxpr/ppermute | solution.py:20
  398.7 19.5 %collective-permute-start = (f32[8,128,128]{2,1,0:T(8,128)}, f32[8,128,128]{2,1,0:T(8,128)S(1)}, u32[]{:S(2)}, u32[]{:S(2)}) collective-permute-start(f32[8,128,128]{2,1,0:T(8,128)} %convolution_add_fusion.9), channel_id=1, source_target_pairs={{0,4},{4,8},{8,12},{12,16},{16,20},{20,24},{24,28},{28,32},{32,36}... | collective-permute-start | bytes 1572872 | tf_op jit(solution)/shard_map/while/body/eval_jaxpr/ppermute | solution.py:20
  420.7 17.8 %collective-permute-start = (f32[8,128,128]{2,1,0:T(8,128)}, f32[8,128,128]{2,1,0:T(8,128)S(1)}, u32[]{:S(2)}, u32[]{:S(2)}) collective-permute-start(f32[8,128,128]{2,1,0:T(8,128)} %convolution_add_fusion.9), channel_id=1, source_target_pairs={{0,4},{4,8},{8,12},{12,16},{16,20},{20,24},{24,28},{28,32},{32,36}... | collective-permute-start | bytes 1572872 | tf_op jit(solution)/shard_map/while/body/eval_jaxpr/ppermute | solution.py:20
  441.0 15.4 %collective-permute-start = (f32[8,128,128]{2,1,0:T(8,128)}, f32[8,128,128]{2,1,0:T(8,128)S(1)}, u32[]{:S(2)}, u32[]{:S(2)}) collective-permute-start(f32[8,128,128]{2,1,0:T(8,128)} %convolution_add_fusion.9), channel_id=1, source_target_pairs={{0,4},{4,8},{8,12},{12,16},{16,20},{20,24},{24,28},{28,32},{32,36}... | collective-permute-start | bytes 1572872 | tf_op jit(solution)/shard_map/while/body/eval_jaxpr/ppermute | solution.py:20
  458.9 15.2 %collective-permute-start = (f32[8,128,128]{2,1,0:T(8,128)}, f32[8,128,128]{2,1,0:T(8,128)S(1)}, u32[]{:S(2)}, u32[]{:S(2)}) collective-permute-start(f32[8,128,128]{2,1,0:T(8,128)} %convolution_add_fusion.9), channel_id=1, source_target_pairs={{0,4},{4,8},{8,12},{12,16},{16,20},{20,24},{24,28},{28,32},{32,36}... | collective-permute-start | bytes 1572872 | tf_op jit(solution)/shard_map/while/body/eval_jaxpr/ppermute | solution.py:20
  476.6 14.3 %collective-permute-start = (f32[8,128,128]{2,1,0:T(8,128)}, f32[8,128,128]{2,1,0:T(8,128)S(1)}, u32[]{:S(2)}, u32[]{:S(2)}) collective-permute-start(f32[8,128,128]{2,1,0:T(8,128)} %convolution_add_fusion.9), channel_id=1, source_target_pairs={{0,4},{4,8},{8,12},{12,16},{16,20},{20,24},{24,28},{28,32},{32,36}... | collective-permute-start | bytes 1572872 | tf_op jit(solution)/shard_map/while/body/eval_jaxpr/ppermute | solution.py:20
  493.5 13.4 %collective-permute-start = (f32[8,128,128]{2,1,0:T(8,128)}, f32[8,128,128]{2,1,0:T(8,128)S(1)}, u32[]{:S(2)}, u32[]{:S(2)}) collective-permute-start(f32[8,128,128]{2,1,0:T(8,128)} %convolution_add_fusion.9), channel_id=1, source_target_pairs={{0,4},{4,8},{8,12},{12,16},{16,20},{20,24},{24,28},{28,32},{32,36}... | collective-permute-start | bytes 1572872 | tf_op jit(solution)/shard_map/while/body/eval_jaxpr/ppermute | solution.py:20
  509.4 13.4 %collective-permute-start = (f32[8,128,128]{2,1,0:T(8,128)}, f32[8,128,128]{2,1,0:T(8,128)S(1)}, u32[]{:S(2)}, u32[]{:S(2)}) collective-permute-start(f32[8,128,128]{2,1,0:T(8,128)} %convolution_add_fusion.9), channel_id=1, source_target_pairs={{0,4},{4,8},{8,12},{12,16},{16,20},{20,24},{24,28},{28,32},{32,36}... | collective-permute-start | bytes 1572872 | tf_op jit(solution)/shard_map/while/body/eval_jaxpr/ppermute | solution.py:20
  525.3 13.4 %collective-permute-start = (f32[8,128,128]{2,1,0:T(8,128)}, f32[8,128,128]{2,1,0:T(8,128)S(1)}, u32[]{:S(2)}, u32[]{:S(2)}) collective-permute-start(f32[8,128,128]{2,1,0:T(8,128)} %convolution_add_fusion.9), channel_id=1, source_target_pairs={{0,4},{4,8},{8,12},{12,16},{16,20},{20,24},{24,28},{28,32},{32,36}... | collective-permute-start | bytes 1572872 | tf_op jit(solution)/shard_map/while/body/eval_jaxpr/ppermute | solution.py:20
  541.2 14.0 %collective-permute-start = (f32[8,128,128]{2,1,0:T(8,128)}, f32[8,128,128]{2,1,0:T(8,128)S(1)}, u32[]{:S(2)}, u32[]{:S(2)}) collective-permute-start(f32[8,128,128]{2,1,0:T(8,128)} %convolution_add_fusion.9), channel_id=1, source_target_pairs={{0,4},{4,8},{8,12},{12,16},{16,20},{20,24},{24,28},{28,32},{32,36}... | collective-permute-start | bytes 1572872 | tf_op jit(solution)/shard_map/while/body/eval_jaxpr/ppermute | solution.py:20
  557.7 14.3 %collective-permute-start = (f32[8,128,128]{2,1,0:T(8,128)}, f32[8,128,128]{2,1,0:T(8,128)S(1)}, u32[]{:S(2)}, u32[]{:S(2)}) collective-permute-start(f32[8,128,128]{2,1,0:T(8,128)} %convolution_add_fusion.9), channel_id=1, source_target_pairs={{0,4},{4,8},{8,12},{12,16},{16,20},{20,24},{24,28},{28,32},{32,36}... | collective-permute-start | bytes 1572872 | tf_op jit(solution)/shard_map/while/body/eval_jaxpr/ppermute | solution.py:20
  574.5 14.3 %collective-permute-start = (f32[8,128,128]{2,1,0:T(8,128)}, f32[8,128,128]{2,1,0:T(8,128)S(1)}, u32[]{:S(2)}, u32[]{:S(2)}) collective-permute-start(f32[8,128,128]{2,1,0:T(8,128)} %convolution_add_fusion.9), channel_id=1, source_target_pairs={{0,4},{4,8},{8,12},{12,16},{16,20},{20,24},{24,28},{28,32},{32,36}... | collective-permute-start | bytes 1572872 | tf_op jit(solution)/shard_map/while/body/eval_jaxpr/ppermute | solution.py:20
  591.3 14.3 %collective-permute-start = (f32[8,128,128]{2,1,0:T(8,128)}, f32[8,128,128]{2,1,0:T(8,128)S(1)}, u32[]{:S(2)}, u32[]{:S(2)}) collective-permute-start(f32[8,128,128]{2,1,0:T(8,128)} %convolution_add_fusion.9), channel_id=1, source_target_pairs={{0,4},{4,8},{8,12},{12,16},{16,20},{20,24},{24,28},{28,32},{32,36}... | collective-permute-start | bytes 1572872 | tf_op jit(solution)/shard_map/while/body/eval_jaxpr/ppermute | solution.py:20
  608.1 14.8 %collective-permute-start = (f32[8,128,128]{2,1,0:T(8,128)}, f32[8,128,128]{2,1,0:T(8,128)S(1)}, u32[]{:S(2)}, u32[]{:S(2)}) collective-permute-start(f32[8,128,128]{2,1,0:T(8,128)} %convolution_add_fusion.9), channel_id=1, source_target_pairs={{0,4},{4,8},{8,12},{12,16},{16,20},{20,24},{24,28},{28,32},{32,36}... | collective-permute-start | bytes 1572872 | tf_op jit(solution)/shard_map/while/body/eval_jaxpr/ppermute | solution.py:20
  625.4 16.1 %collective-permute-start = (f32[8,128,128]{2,1,0:T(8,128)}, f32[8,128,128]{2,1,0:T(8,128)S(1)}, u32[]{:S(2)}, u32[]{:S(2)}) collective-permute-start(f32[8,128,128]{2,1,0:T(8,128)} %convolution_add_fusion.9), channel_id=1, source_target_pairs={{0,4},{4,8},{8,12},{12,16},{16,20},{20,24},{24,28},{28,32},{32,36}... | collective-permute-start | bytes 1572872 | tf_op jit(solution)/shard_map/while/body/eval_jaxpr/ppermute | solution.py:20
  644.1 17.8 %collective-permute-start = (f32[8,128,128]{2,1,0:T(8,128)}, f32[8,128,128]{2,1,0:T(8,128)S(1)}, u32[]{:S(2)}, u32[]{:S(2)}) collective-permute-start(f32[8,128,128]{2,1,0:T(8,128)} %convolution_add_fusion.9), channel_id=1, source_target_pairs={{0,4},{4,8},{8,12},{12,16},{16,20},{20,24},{24,28},{28,32},{32,36}... | collective-permute-start | bytes 1572872 | tf_op jit(solution)/shard_map/while/body/eval_jaxpr/ppermute | solution.py:20
  664.4 15.4 %collective-permute-start = (f32[8,128,128]{2,1,0:T(8,128)}, f32[8,128,128]{2,1,0:T(8,128)S(1)}, u32[]{:S(2)}, u32[]{:S(2)}) collective-permute-start(f32[8,128,128]{2,1,0:T(8,128)} %convolution_add_fusion.9), channel_id=1, source_target_pairs={{0,4},{4,8},{8,12},{12,16},{16,20},{20,24},{24,28},{28,32},{32,36}... | collective-permute-start | bytes 1572872 | tf_op jit(solution)/shard_map/while/body/eval_jaxpr/ppermute | solution.py:20
  682.4 15.2 %collective-permute-start = (f32[8,128,128]{2,1,0:T(8,128)}, f32[8,128,128]{2,1,0:T(8,128)S(1)}, u32[]{:S(2)}, u32[]{:S(2)}) collective-permute-start(f32[8,128,128]{2,1,0:T(8,128)} %convolution_add_fusion.9), channel_id=1, source_target_pairs={{0,4},{4,8},{8,12},{12,16},{16,20},{20,24},{24,28},{28,32},{32,36}... | collective-permute-start | bytes 1572872 | tf_op jit(solution)/shard_map/while/body/eval_jaxpr/ppermute | solution.py:20
  697.6 2.8 copy-start.14
  701.9 2.0 copy-start.15
  703.9 2.8 copy-start.14
  708.1 2.0 copy-start.15
  710.1 2.8 copy-start.14
  714.4 2.0 copy-start.15
  716.4 2.8 copy-start.14
  720.7 2.0 copy-start.15
  727.8 82.8 %copy-start.11 = (bf16[128,2304]{1,0:T(8,128)(2,1)S(1)}, bf16[128,2304]{1,0:T(8,128)(2,1)}, u32[]{:S(2)}) copy-start(bf16[128,2304]{1,0:T(8,128)(2,1)} %param.26) | copy-start | bytes 1769476
  727.8 84.3 %copy-start.26 = (f32[2304]{0:T(1024)S(1)}, f32[2304]{0:T(1024)}, u32[]{:S(2)}) copy-start(f32[2304]{0:T(1024)} %param.27) | copy-start | bytes 27652
  727.9 242.8 %all-gather.2.cloned.1.call-start = ((), (), s32[]{:S(2)}) async-start(), calls=%async_computation.1 | async-start | bytes 4325376 | tf_op jit(solution)/shard_map/all_gather | solution.py:194
  813.8 156.9 %copy-start.10 = (bf16[512,2,512]{2,1,0:T(2,128)(2,1)S(1)}, bf16[512,2,512]{2,1,0:T(2,128)(2,1)}, u32[]{:S(2)}) copy-start(bf16[512,2,512]{2,1,0:T(2,128)(2,1)} %param.31) | copy-start | bytes 3145732
  1001.5 1.2 copy-start.17
  1047.7 1.2 copy-start.17
  (10 other events, 10.5 us)
Sparse Core Ops, SparseCore 0:
  728.0 82.5 all-reduce.1
  813.9 156.7 all-gather.1
where the time goes:
time: 1080 us; the launch traced here: 1070 us
  waiting for transfers between devices  498 us (46%)
  starting transfers between devices  205 us (19%)
  matrix products  186 us (17%)
  other arithmetic  119 us (11%)
  local copies, waits for them, and re-layouts  44.7 us (4%)
  between operations  14.4 us (1%)
    ppermute x32, waiting for transfers between devices, passed_along(): return lax.ppermute(block, axis, route)  260 us
    ppermute x32, starting transfers between devices, passed_along(): return lax.ppermute(block, axis, route)  205 us
    all_gather x1, waiting for transfers between devices, per_device(): piece = lax.all_gather(latent, 'ctx', axis=0, tiled=True)  154 us
    dot_general x43, matrix products, matmul_heads(): return jnp.einsum('hij,hjk->hik', left, right, precision=highest_precision)  99.9 us
    psum x1, waiting for transfers between devices, per_device(): summed = lax.psum(partial_proj, 'head')  82.7 us
    another operation x4, other arithmetic, delta_rule(): jax.scipy.linalg.solve_triangular(system, jnp.concatenate([values_new, ke...  81.5 us
    dot_general x8, matrix products, one_block(): jnp.dot(latent_block, flat_up, preferred_element_type=jnp.float32)  24.7 us
  transfers between devices with their start and end apart: 34, of which 33 were waited for; matrix products, arithmetic and copies ran while one was open for 2% of the time, Pallas kernels for 0%

commit v1 on v0

--- a/solution.py
+++ b/solution.py
@@ -55,6 +55,25 @@
 
 def matmul_heads(left, right):
     return jnp.einsum("hij,hjk->hik", left, right, precision=highest_precision)
+
+
+def matmul_batched(left, right):
+    return jnp.einsum("...ij,...jk->...ik", left, right, precision=highest_precision)
+
+
+def unit_lower_inverse(system):
+    size = system.shape[-1]
+    rows = jnp.arange(size)[:, None]
+    cols = jnp.arange(size)[None, :]
+    inverse = jnp.broadcast_to(jnp.eye(size, dtype=system.dtype), system.shape)
+    width = 1
+    while width < size:
+        below = (rows // (2 * width) == cols // (2 * width)) & (rows // width != cols // width)
+        off_block = jnp.where(below, system, 0.0)
+        correction = matmul_batched(matmul_batched(inverse, off_block), inverse)
+        inverse = inverse - lax.optimization_barrier(correction)
+        width *= 2
+    return inverse
 
 
 def delta_rule(kda_query, kda_key, kda_value, gate_log, beta):
@@ -80,8 +99,8 @@
         * strict
     )
     system = coupling + jnp.eye(span_rows, dtype=jnp.float32)
-    solved = jax.scipy.linalg.solve_triangular(
-        system, jnp.concatenate([values_new, keys_grown], axis=-1), lower=True, unit_diagonal=True
+    solved = matmul_batched(
+        unit_lower_inverse(system), jnp.concatenate([values_new, keys_grown], axis=-1)
     )
     fresh = solved[..., :DK] * rates
     carried = solved[..., DK:] * rates
@@ -166,13 +185,19 @@
     device_move, device_shift, span_data = delta_rule(kda_query, kda_key, kda_value, gate_log, beta)
     heads = device_move.shape[0]
 
-    def relay(step_index, incoming):
-        leaving = matmul_heads(device_move, incoming) + device_shift
-        return passed_along(leaving, "ctx", 1)
-
-    start_state = lax.fori_loop(
-        0, lax.axis_size("ctx") - 1, relay, jnp.zeros((heads, DK, DK), jnp.float32)
-    )
+    ctx_size = lax.axis_size("ctx")
+    move, shift = device_move, device_shift
+    distance = 1
+    while distance < ctx_size:
+        shift_in = passed_along(shift, "ctx", distance)
+        if 2 * distance < ctx_size:
+            move_in = passed_along(move, "ctx", distance)
+            shift = matmul_heads(move, shift_in) + shift
+            move = matmul_heads(move, move_in)
+        else:
+            shift = matmul_heads(move, shift_in) + shift
+        distance *= 2
+    start_state = passed_along(shift, "ctx", 1)
     kda_core = emit_spans(start_state, span_data)
     partial_proj = jnp.dot(kda_core, kda_out_weight, preferred_element_type=jnp.float32)
     summed = lax.psum(partial_proj, "head")

time: 1080 us -> 580 us (0.54)
  waiting for transfers between devices: 498 us -> 285 us
  starting transfers between devices: 205 us -> 53.7 us
  other arithmetic: 119 us -> 35.1 us
  matrix products: 186 us -> 128 us
    ppermute x32 -> x11, waiting for transfers between devices: 260 us -> 54.5 us  [passed_along(): return lax.ppermute(block, axis, route)]
    ppermute x32 -> x11, starting transfers between devices: 205 us -> 53.4 us  [passed_along(): return lax.ppermute(block, axis, route)]
    another operation x4 -> x0, other arithmetic: 81.5 us -> none  [delta_rule(): jax.scipy.linalg.solve_triangular(system, jnp.concatenate([values_new, ke...]
    dot_general x43 -> x21, matrix products: 99.9 us -> 36.2 us  [matmul_heads(): return jnp.einsum('hij,hjk->hik', left, right, precision=highest_precision)]
  transfers between devices with their start and end apart: 34 -> 13, of which waited for: 33 -> 11; matrix products, arithmetic and copies ran while one was open for 2% -> 4% of each run, Pallas kernels for 0% -> 0%
where the time goes in v1:
time: 580 us; the launch traced here: 568 us
  waiting for transfers between devices  285 us (49%)
  matrix products  128 us (22%)
  starting transfers between devices  53.7 us (9%)
  local copies, waits for them, and re-layouts  45.6 us (8%)
  other arithmetic  35.1 us (6%)
  between operations  15 us (3%)
  loops' own time  5.85 us (1%)
    all_gather x1, waiting for transfers between devices, per_device(): piece = lax.all_gather(latent, 'ctx', axis=0, tiled=True)  154 us
    psum x1, waiting for transfers between devices, per_device(): summed = lax.psum(partial_proj, 'head')  76.8 us
    ppermute x11, waiting for transfers between devices, passed_along(): return lax.ppermute(block, axis, route)  54.5 us
    ppermute x11, starting transfers between devices, passed_along(): return lax.ppermute(block, axis, route)  53.4 us
    dot_general x21, matrix products, matmul_heads(): return jnp.einsum('hij,hjk->hik', left, right, precision=highest_precision)  36.2 us
    dot_general x8, matrix products, one_block(): jnp.dot(latent_block, flat_up, preferred_element_type=jnp.float32)  24.8 us
    dot_general x8, matrix products, one_block(): jnp.einsum('hqk,khd->hqd', weights.astype(jnp.bfloat16), paired[:, 1], pr...  18 us
    reshape x8, local copies, waits for them, and re-layouts, one_block(): paired = jnp.dot(latent_block, flat_up, preferred_element_type=jnp.float3...  14.3 us
  transfers between devices with their start and end apart: 13, of which 11 were waited for; matrix products, arithmetic and copies ran while one was open for 4% of the time, Pallas kernels for 0%

profile of v1, /device:TPU:0, one launch (start us, length us, event | category | flops | bytes accessed | tf_op | source)
XLA Modules:
  0.0 568.4 jit_solution(7206798284100567644)
XLA Ops:
  8.2 3.5 collective-permute-start
  12.9 7.6 %fusion.53 = f32[4,8,32,128]{3,1,2,0:T(8,128)S(1)} fusion(f32[4,32,8,128]{3,2,1,0:T(8,128)S(1)} %bitcast.233), kind=kOutput, calls=%fused_computation.91 | output fusion | flops 4063232 | bytes 1048576 | tf_op jit(solution)/shard_map/jit(cumsum)/reduce_window_sum | solution.py:86
  47.0 4.8 fusion.91
  51.9 5.2 multiply_subtract_fusion
  57.1 18.1 %while.41 = (s32[]{:T(128)}, f32[8,128,128]{2,1,0:T(8,128)S(1)}, f32[8,128,128]{2,1,0:T(8,128)}, f32[4,8,128,128]{3,2,1,0:T(8,128)}, f32[4,8,128,128]{3,2,1,0:T(8,128)}, /*index=5*/s32[]{:T(128)}, s32[]{:T(128)}) while((s32[]{:T(128)}, f32[8,128,128]{2,1,0:T(8,128)S(1)}, f32[8,128,128]{2,1,0:T(8,128)}, ...), condition=%wide.region_3.4_spmd.clone, body=%wide.region_2.3_spmd.clone.sunk | while | flops 402915328 | bytes 7865982 | solution.py:129
  59.0 2.6 convolution_add_fusion.13
  63.5 2.6 convolution_add_fusion.13
  68.0 2.6 convolution_add_fusion.13
  72.6 2.6 convolution_add_fusion.13
  75.2 3.4 collective-permute-start.5
  78.6 3.1 collective-permute-start.1
  81.7 9.5 %collective-permute-done.5 = f32[8,128,128]{2,1,0:T(8,128)S(1)} collective-permute-done((f32[8,128,128]{2,1,0:T(8,128)}, f32[8,128,128]{2,1,0:T(8,128)S(1)}, u32[]{:S(2)}, u32[]{:S(2)}) %collective-permute-start.5) | collective-permute-done | bytes 524320 | tf_op jit(solution)/shard_map/ppermute | solution.py:20
  92.9 5.6 collective-permute-start.6
  98.5 3.9 collective-permute-done.1
  103.0 5.6 collective-permute-start.2
  108.6 5.0 collective-permute-done.6
  114.3 7.0 %collective-permute-start.7 = (f32[8,128,128]{2,1,0:T(8,128)S(1)}, f32[8,128,128]{2,1,0:T(8,128)S(1)}, u32[]{:S(2)}, u32[]{:S(2)}) collective-permute-start(f32[8,128,128]{2,1,0:T(8,128)S(1)} %convolution_add_fusion.7), channel_id=1, source_target_pairs={{0,16},{4,20},{8,24},{12,28},{16,32},{20,36},{24,40},{28,44},{32,4... | collective-permute-start | bytes 1572872 | tf_op jit(solution)/shard_map/ppermute | solution.py:20
  121.2 2.2 collective-permute-done.2
  124.0 7.1 %collective-permute-start.3 = (f32[8,128,128]{2,1,0:T(8,128)S(1)}, f32[8,128,128]{2,1,0:T(8,128)S(1)}, u32[]{:S(2)}, u32[]{:S(2)}) collective-permute-start(f32[8,128,128]{2,1,0:T(8,128)S(1)} %fusion.111), channel_id=1, source_target_pairs={{0,16},{4,20},{8,24},{12,28},{16,32},{20,36},{24,40},{28,44},{32,4... | collective-permute-start | bytes 1572872 | tf_op jit(solution)/shard_map/ppermute | solution.py:20
  131.1 6.1 %collective-permute-done.7 = f32[8,128,128]{2,1,0:T(8,128)S(1)} collective-permute-done((f32[8,128,128]{2,1,0:T(8,128)S(1)}, f32[8,128,128]{2,1,0:T(8,128)S(1)}, u32[]{:S(2)}, u32[]{:S(2)}) %collective-permute-start.7) | collective-permute-done | bytes 524320 | tf_op jit(solution)/shard_map/ppermute | solution.py:20
  137.9 5.0 collective-permute-start.8
  142.9 5.5 collective-permute-done.3
  149.0 5.1 collective-permute-start.4
  154.8 6.1 %collective-permute-start.9 = (f32[8,128,128]{2,1,0:T(8,128)S(1)}, f32[8,128,128]{2,1,0:T(8,128)S(1)}, u32[]{:S(2)}, u32[]{:S(2)}) collective-permute-start(f32[8,128,128]{2,1,0:T(8,128)S(1)} %convolution_add_fusion.5), channel_id=1, source_target_pairs={{0,64},{4,68},{8,72},{12,76},{16,80},{20,84},{24,88},{28,92},{32,9... | collective-permute-start | bytes 1572872 | tf_op jit(solution)/shard_map/ppermute | solution.py:20
  161.0 5.4 collective-permute-done.4
  167.0 9.6 %collective-permute-done.9 = f32[8,128,128]{2,1,0:T(8,128)S(1)} collective-permute-done((f32[8,128,128]{2,1,0:T(8,128)S(1)}, f32[8,128,128]{2,1,0:T(8,128)S(1)}, u32[]{:S(2)}, u32[]{:S(2)}) %collective-permute-start.9) | collective-permute-done | bytes 524320 | tf_op jit(solution)/shard_map/ppermute | solution.py:20
  178.1 2.1 collective-permute-start.10
  180.2 2.9 convolution_multiply_fusion.1
  183.1 7.3 %collective-permute-done.10 = f32[8,128,128]{2,1,0:T(8,128)} collective-permute-done((f32[8,128,128]{2,1,0:T(8,128)}, f32[8,128,128]{2,1,0:T(8,128)}, u32[]{:S(2)}, u32[]{:S(2)}) %collective-permute-start.10) | collective-permute-done | bytes 524320 | tf_op jit(solution)/shard_map/ppermute | solution.py:20
  190.4 32.1 %while.40 = (s32[]{:T(128)}, f32[8,128,128]{2,1,0:T(8,128)}, bf16[4,8,32,128]{3,2,1,0:T(8,128)(2,1)}, f32[4,8,128,128]{3,2,1,0:T(8,128)}, f32[4,8,128,128]{3,2,1...) while((s32[]{:T(128)}, f32[8,128,128]{2,1,0:T(8,128)}, ...), condition=%wide.region_6.7_spmd, body=%wide.region_5.6_spmd.sunk | while | flops 314769408 | bytes 7474345 | solution.py:149
  195.6 2.7 convolution_add_fusion.12
  203.7 2.7 convolution_add_fusion.12
  211.7 2.7 convolution_add_fusion.12
  219.7 2.7 convolution_add_fusion.12
  223.5 4.1 fusion.69
  228.0 76.8 %all-reduce.2.cloned.1.call-done = f32[128,2304]{1,0:T(8,128)} async-done(((f32[128,2304]{1,0:T(8,128)}), f32[128,2304]{1,0:T(8,128)}) %all-reduce.2.cloned.1.call-update) | async-done | bytes 1179664 | tf_op jit(solution)/shard_map/psum | solution.py:203
  307.9 3.1 convolution_convert_fusion.1
  311.0 153.8 %all-gather.2.cloned.1.call-done = bf16[4096,512]{1,0:T(8,128)(2,1)} async-done(((bf16[128,512]{1,0:T(8,128)(2,1)}), bf16[4096,512]{1,0:T(8,128)(2,1)}) %all-gather.2.cloned.1.call-update) | async-done | bytes 4194320 | tf_op jit(solution)/shard_map/all_gather | solution.py:219
  464.8 94.8 %conditional.1 = (f32[4,128]{1,0:T(4,128)}, f32[4,128,128]{2,1,0:T(8,128)}) conditional(s32[]{:T(128)} %convert_element_type.95, () %tuple.30, (bf16[4096,512]{1,0:T(8,128)(2,1)}, bf16[512,2,512]{2,1,0:T(2,128)(2,1)S(1)}, bf16[128,512]{1,0:T(8,128)(2,1)}, s32[]{:T(128)}, s32[128]{0:T(128)S(1)}) %tuple.112), branch_computations={%region_10.11_spmd, %region_11.16_spmd} | conditional | flops 674237568 | bytes 15112033 | solution.py:254
  467.9 91.7 %while.39 = (s32[]{:T(128)}, f32[4,128]{1,0:T(4,128)S(1)}, f32[4,128]{1,0:T(4,128)}, f32[4,128,128]{2,1,0:T(8,128)}, s32[8]{0:T(128)S(1)}, /*index=5*/s32[128]{0...) while((s32[]{:T(128)}, f32[4,128]{1,0:T(4,128)S(1)}, ...), condition=%wide.region_15.15_spmd.clone, body=%wide.region_12.14_spmd.clone.sunk | while | flops 674237440 | bytes 12489413 | solution.py:250
  469.3 3.1 convolution_convert_fusion.3
  472.4 1.8 reshape.511
  476.5 2.2 convolution_add_fusion.14
  480.1 3.1 convolution_convert_fusion.3
  483.2 1.8 reshape.511
  488.0 2.3 convolution_add_fusion.14
  491.7 3.1 convolution_convert_fusion.3
  494.8 1.8 reshape.511
  499.6 2.3 convolution_add_fusion.14
  503.2 3.1 convolution_convert_fusion.3
  506.3 1.8 reshape.511
  511.1 2.3 convolution_add_fusion.14
  514.8 3.1 convolution_convert_fusion.3
  517.9 1.8 reshape.511
  522.7 2.3 convolution_add_fusion.14
  526.3 3.1 convolution_convert_fusion.3
  529.4 1.8 reshape.511
  534.2 2.3 convolution_add_fusion.14
  537.9 3.1 convolution_convert_fusion.3
  541.0 1.8 reshape.511
  545.8 2.3 convolution_add_fusion.14
  549.4 3.1 convolution_convert_fusion.3
  552.5 1.8 reshape.511
  557.3 2.3 convolution_add_fusion.14
  (279 shorter events, 102.6 us)
Async XLA Ops:
  7.2 299.1 %copy-start = (bf16[2304,512]{1,0:T(8,128)(2,1)S(1)}, bf16[2304,512]{1,0:T(8,128)(2,1)}, u32[]{:S(2)}) copy-start(bf16[2304,512]{1,0:T(8,128)(2,1)} %param.26) | copy-start | bytes 7077892
  7.2 14.7 %copy-start.20 = (f32[3,4,1024]{2,1,0:T(4,128)S(1)}, f32[3,4,1024]{2,1,0:T(4,128)}, u32[]{:S(2)}) copy-start(f32[3,4,1024]{2,1,0:T(4,128)} %param.22) | copy-start | bytes 147460
  7.2 16.1 %copy-start.26 = (f32[128,8]{0,1:T(8,128)S(1)}, f32[128,8]{0,1:T(8,128)}, u32[]{:S(2)}) copy-start(f32[128,8]{0,1:T(8,128)} %param.21) | copy-start | bytes 12292
  7.2 297.5 %all-reduce.2.cloned.1.call-start = ((), (), s32[]{:S(2)}) async-start(), calls=%async_computation | async-start | bytes 2359296 | tf_op jit(solution)/shard_map/psum | solution.py:203
  8.2 15.8 %collective-permute-start = (bf16[3,3,1024]{2,1,0:T(4,128)(2,1)S(1)}, bf16[3,3,1024]{2,1,0:T(4,128)(2,1)S(1)}, u32[]{:S(2)}, u32[]{:S(2)}) collective-permute-start(bf16[3,3,1024]{2,1,0:T(4,128)(2,1)S(1)} %slice.54), channel_id=1, source_target_pairs={{0,4},{4,8},{8,12},{12,16},{16,20},{20,24},{24,28},{28,32},{32,36}... | collective-permute-start | bytes 55304 | tf_op jit(solution)/shard_map/ppermute | solution.py:20
  20.5 31.3 %copy-start.1 = (f32[4,8,32,128]{3,1,2,0:T(8,128)}, f32[4,8,32,128]{3,1,2,0:T(8,128)S(1)}, u32[]{:S(2)}) copy-start(f32[4,8,32,128]{3,1,2,0:T(8,128)S(1)} %fusion.53) | copy-start | bytes 1572868
  26.3 1.8 copy-start.6
  34.6 1.0 copy-start.9
  35.5 16.3 %copy-start.3 = (f32[16,8,8,128]{3,2,1,0:T(8,128)}, f32[16,8,8,128]{3,2,1,0:T(8,128)S(1)}, u32[]{:S(2)}) copy-start(f32[16,8,8,128]{3,2,1,0:T(8,128)S(1)} %copy.48) | copy-start | bytes 1572868
  35.8 1.1 copy-start.16
  35.8 1.1 copy-start.19
  36.9 1.1 copy-start.25
  38.0 1.2 copy-start.24
  39.9 0.8 copy-start.23
  41.3 0.8 copy-start.22
  42.7 0.8 copy-start.21
  46.3 0.7 copy-start.15
  46.5 5.3 copy-start.7
  46.5 5.3 copy-start.8
  47.0 4.8 copy-start.18
  57.1 1.8 copy-start.5
  61.7 1.8 copy-start.5
  66.2 1.8 copy-start.5
  70.7 1.8 copy-start.5
  75.2 16.1 %collective-permute-start.5 = (f32[8,128,128]{2,1,0:T(8,128)}, f32[8,128,128]{2,1,0:T(8,128)S(1)}, u32[]{:S(2)}, u32[]{:S(2)}) collective-permute-start(f32[8,128,128]{2,1,0:T(8,128)} %get-tuple-element.148), channel_id=1, source_target_pairs={{0,4},{4,8},{8,12},{12,16},{16,20},{20,24},{24,28},{28,32},{32,36}... | collective-permute-start | bytes 1572872 | tf_op jit(solution)/shard_map/ppermute | solution.py:20
  78.6 23.8 %collective-permute-start.1 = (f32[8,128,128]{2,1,0:T(8,128)S(1)}, f32[8,128,128]{2,1,0:T(8,128)S(1)}, u32[]{:S(2)}, u32[]{:S(2)}) collective-permute-start(f32[8,128,128]{2,1,0:T(8,128)S(1)} %get-tuple-element.147), channel_id=1, source_target_pairs={{0,4},{4,8},{8,12},{12,16},{16,20},{20,24},{24,28},{28,32},{32,36}... | collective-permute-start | bytes 1572872 | tf_op jit(solution)/shard_map/ppermute | solution.py:20
  92.9 20.7 %collective-permute-start.6 = (f32[8,128,128]{2,1,0:T(8,128)S(1)}, f32[8,128,128]{2,1,0:T(8,128)S(1)}, u32[]{:S(2)}, u32[]{:S(2)}) collective-permute-start(f32[8,128,128]{2,1,0:T(8,128)S(1)} %convolution_add_fusion.8), channel_id=1, source_target_pairs={{0,8},{4,12},{8,16},{12,20},{16,24},{20,28},{24,32},{28,36},{32,40... | collective-permute-start | bytes 1572872 | tf_op jit(solution)/shard_map/ppermute | solution.py:20
  103.0 20.4 %collective-permute-start.2 = (f32[8,128,128]{2,1,0:T(8,128)S(1)}, f32[8,128,128]{2,1,0:T(8,128)S(1)}, u32[]{:S(2)}, u32[]{:S(2)}) collective-permute-start(f32[8,128,128]{2,1,0:T(8,128)S(1)} %fusion.110), channel_id=1, source_target_pairs={{0,8},{4,12},{8,16},{12,20},{16,24},{20,28},{24,32},{28,36},{32,40... | collective-permute-start | bytes 1572872 | tf_op jit(solution)/shard_map/ppermute | solution.py:20
  114.3 23.0 %collective-permute-start.7 = (f32[8,128,128]{2,1,0:T(8,128)S(1)}, f32[8,128,128]{2,1,0:T(8,128)S(1)}, u32[]{:S(2)}, u32[]{:S(2)}) collective-permute-start(f32[8,128,128]{2,1,0:T(8,128)S(1)} %convolution_add_fusion.7), channel_id=1, source_target_pairs={{0,16},{4,20},{8,24},{12,28},{16,32},{20,36},{24,40},{28,44},{32,4... | collective-permute-start | bytes 1572872 | tf_op jit(solution)/shard_map/ppermute | solution.py:20
  124.0 24.4 %collective-permute-start.3 = (f32[8,128,128]{2,1,0:T(8,128)S(1)}, f32[8,128,128]{2,1,0:T(8,128)S(1)}, u32[]{:S(2)}, u32[]{:S(2)}) collective-permute-start(f32[8,128,128]{2,1,0:T(8,128)S(1)} %fusion.111), channel_id=1, source_target_pairs={{0,16},{4,20},{8,24},{12,28},{16,32},{20,36},{24,40},{28,44},{32,4... | collective-permute-start | bytes 1572872 | tf_op jit(solution)/shard_map/ppermute | solution.py:20
  137.9 16.2 %collective-permute-start.8 = (f32[8,128,128]{2,1,0:T(8,128)S(1)}, f32[8,128,128]{2,1,0:T(8,128)S(1)}, u32[]{:S(2)}, u32[]{:S(2)}) collective-permute-start(f32[8,128,128]{2,1,0:T(8,128)S(1)} %convolution_add_fusion.6), channel_id=1, source_target_pairs={{0,32},{4,36},{8,40},{12,44},{16,48},{20,52},{24,56},{28,60},{32,6... | collective-permute-start | bytes 1572872 | tf_op jit(solution)/shard_map/ppermute | solution.py:20
  149.0 17.3 %collective-permute-start.4 = (f32[8,128,128]{2,1,0:T(8,128)S(1)}, f32[8,128,128]{2,1,0:T(8,128)S(1)}, u32[]{:S(2)}, u32[]{:S(2)}) collective-permute-start(f32[8,128,128]{2,1,0:T(8,128)S(1)} %fusion.112), channel_id=1, source_target_pairs={{0,32},{4,36},{8,40},{12,44},{16,48},{20,52},{24,56},{28,60},{32,6... | collective-permute-start | bytes 1572872 | tf_op jit(solution)/shard_map/ppermute | solution.py:20
  154.8 25.4 %copy-start.2 = (f32[4,8,32,128]{3,1,2,0:T(8,128)S(1)}, f32[4,8,32,128]{3,1,2,0:T(8,128)}, u32[]{:S(2)}) copy-start(f32[4,8,32,128]{3,1,2,0:T(8,128)} %copy-done.1) | copy-start | bytes 1572868
  154.8 25.4 %copy-start.4 = (f32[16,8,8,128]{3,2,1,0:T(8,128)S(1)}, f32[16,8,8,128]{3,2,1,0:T(8,128)}, u32[]{:S(2)}) copy-start(f32[16,8,8,128]{3,2,1,0:T(8,128)} %copy-done.3) | copy-start | bytes 1572868
  154.8 21.8 %collective-permute-start.9 = (f32[8,128,128]{2,1,0:T(8,128)S(1)}, f32[8,128,128]{2,1,0:T(8,128)S(1)}, u32[]{:S(2)}, u32[]{:S(2)}) collective-permute-start(f32[8,128,128]{2,1,0:T(8,128)S(1)} %convolution_add_fusion.5), channel_id=1, source_target_pairs={{0,64},{4,68},{8,72},{12,76},{16,80},{20,84},{24,88},{28,92},{32,9... | collective-permute-start | bytes 1572872 | tf_op jit(solution)/shard_map/ppermute | solution.py:20
  178.1 12.3 %collective-permute-start.10 = (f32[8,128,128]{2,1,0:T(8,128)}, f32[8,128,128]{2,1,0:T(8,128)}, u32[]{:S(2)}, u32[]{:S(2)}) collective-permute-start(f32[8,128,128]{2,1,0:T(8,128)} %convolution_add_fusion.4), channel_id=1, source_target_pairs={{0,4},{4,8},{8,12},{12,16},{16,20},{20,24},{24,28},{28,32},{32,36}... | collective-permute-start | bytes 1572872 | tf_op jit(solution)/shard_map/ppermute | solution.py:20
  190.4 3.8 copy-start.13
  195.6 2.8 copy-start.14
  198.4 3.8 copy-start.13
  203.7 2.8 copy-start.14
  206.4 3.8 copy-start.13
  211.7 2.8 copy-start.14
  214.4 3.8 copy-start.13
  219.7 2.8 copy-start.14
  227.7 77.1 %copy-start.11 = (bf16[128,2304]{1,0:T(8,128)(2,1)S(1)}, bf16[128,2304]{1,0:T(8,128)(2,1)}, u32[]{:S(2)}) copy-start(bf16[128,2304]{1,0:T(8,128)(2,1)} %param.24) | copy-start | bytes 1769476
  227.7 78.6 %copy-start.28 = (f32[2304]{0:T(1024)S(1)}, f32[2304]{0:T(1024)}, u32[]{:S(2)}) copy-start(f32[2304]{0:T(1024)} %param.25) | copy-start | bytes 27652
  227.7 237.1 %all-gather.2.cloned.1.call-start = ((), (), s32[]{:S(2)}) async-start(), calls=%async_computation.1 | async-start | bytes 4325376 | tf_op jit(solution)/shard_map/all_gather | solution.py:219
  306.3 0.8 copy-start.12
  306.3 0.8 copy-start.27
  307.9 156.9 %copy-start.10 = (bf16[512,2,512]{2,1,0:T(2,128)(2,1)S(1)}, bf16[512,2,512]{2,1,0:T(2,128)(2,1)}, u32[]{:S(2)}) copy-start(bf16[512,2,512]{2,1,0:T(2,128)(2,1)} %param.29) | copy-start | bytes 3145732
  474.2 1.2 copy-start.17
  485.0 1.2 copy-start.17
  496.6 1.2 copy-start.17
  508.1 1.2 copy-start.17
  519.7 1.2 copy-start.17
  531.2 1.2 copy-start.17
  542.8 1.2 copy-start.17
  554.3 1.2 copy-start.17
Sparse Core Ops, SparseCore 0:
  227.8 76.8 all-reduce.1
  308.0 156.7 all-gather.1
